TPU v7x, 32 devices: a whole 2x2x4 slice. The times are simulated.
32 devices in a mesh: dp: 2 (over x), fsdp: 16 (over z, y, core).
Axes of the slice: x: 2, y: 2, z: 4, core: 2. Of those that a mesh axis runs over, the one named last changes fastest.
Arguments:
- tokens: bfloat16 [32, 512, 1024], P(('dp', 'fsdp')), may hold values from -6 to 6
- lengths: int32 [32], P(('dp', 'fsdp')), may hold values from 128 to 512, as said below
- time_embed: bfloat16 [32, 256], P(('dp', 'fsdp')), may hold values from -6 to 6
- cotangent: bfloat16 [32, 512, 1024], P(('dp', 'fsdp')), may hold values from -6 to 6
- time_weight: bfloat16 [256, 1024], P('fsdp'), may hold values from -0.1875 to 0.1875
- attn_gain: bfloat16 [1024], P('fsdp'), may hold values from 0.099609375 to 1.8984375
- attn_shift: bfloat16 [1024], P('fsdp'), may hold values from -3 to 3
- qkv_weight: bfloat16 [1024, 3072], P('fsdp'), may hold values from -0.1875 to 0.1875
- out_weight: bfloat16 [1024, 1024], P('fsdp'), may hold values from -0.75 to 0.75
- mlp_gain: bfloat16 [1024], P('fsdp'), may hold values from 0.099609375 to 1.8984375
- mlp_shift: bfloat16 [1024], P('fsdp'), may hold values from -3 to 3
- up_weight: bfloat16 [1024, 4096], P('fsdp'), may hold values from -0.1875 to 0.1875
- up_bias: bfloat16 [4096], P('fsdp'), may hold values from -3 to 3
- down_weight: bfloat16 [4096, 1024], P('fsdp'), may hold values from -0.09375 to 0.09375
- down_bias: bfloat16 [1024], P('fsdp'), may hold values from -3 to 3
Outputs:
- layer_out: bfloat16 [32, 512, 1024], P(('dp', 'fsdp'))
- token_grad: bfloat16 [32, 512, 1024], P(('dp', 'fsdp'))
- time_weight_grad: float32 [256, 1024], P('fsdp')
- attn_gain_grad: float32 [1024], P('fsdp')
- attn_shift_grad: float32 [1024], P('fsdp')
- qkv_weight_grad: float32 [1024, 3072], P('fsdp')
- out_weight_grad: float32 [1024, 1024], P('fsdp')
- mlp_gain_grad: float32 [1024], P('fsdp')
- mlp_shift_grad: float32 [1024], P('fsdp')
- up_weight_grad: float32 [1024, 4096], P('fsdp')
- up_bias_grad: float32 [4096], P('fsdp')
- down_weight_grad: float32 [4096, 1024], P('fsdp')
- down_bias_grad: float32 [1024], P('fsdp')
Inputs may be any that keep to these rules, and one draw needn't show every extreme that they name: `lengths`: each sequence's count of real tokens; one sequence of every draw has 512.
All inputs are finite; a program needn't handle non-finite values.
Results may differ from a plain program's by a relative error of at most 0.02.
Values may be sent and summed in bfloat16 or wider, within the bound.
No kernel may reach another device: no remote copies, remote signals or barrier semaphores. Data moves between devices by JAX's collectives and lax.ppermute only.
A program may use at most 192 MiB of HBM per device.

v0:
```python
import math
import jax
import jax.numpy as jnp
from jax import lax
from jax.sharding import PartitionSpec as P

HEADS = 16
HD = 64


def normalize(values_in):
    center = values_in - jnp.mean(values_in, axis=-1, keepdims=True)
    inverse = lax.rsqrt(jnp.mean(center * center, axis=-1, keepdims=True) + 1e-05)
    return (center * inverse, inverse)


def norm_back(grad_hat, normed, inverse):
    return inverse * (
        grad_hat
        - jnp.mean(grad_hat, axis=-1, keepdims=True)
        - normed * jnp.mean(grad_hat * normed, axis=-1, keepdims=True)
    )


def rotary_tables(length, head_size):
    half_size = head_size // 2
    frequency = jnp.exp(
        jnp.arange(half_size, dtype=jnp.float32) * (-2.0 * math.log(10000.0) / head_size)
    )
    angles = jnp.arange(length, dtype=jnp.float32)[:, None] * frequency[None, :]
    angles = jnp.concatenate([angles, angles], axis=-1)
    return (jnp.cos(angles)[:, None, :], jnp.sin(angles)[:, None, :])


def rotate(values_in, cosine_table, sine_table):
    half_size = values_in.shape[-1] // 2
    turned = jnp.concatenate([-values_in[..., half_size:], values_in[..., :half_size]], axis=-1)
    return values_in * cosine_table + turned * sine_table


def rotate_back(grad_in, cosine_table, sine_table):
    half_size = grad_in.shape[-1] // 2
    sined = grad_in * sine_table
    return grad_in * cosine_table + jnp.concatenate(
        [sined[..., half_size:], -sined[..., :half_size]], axis=-1
    )


def rows_dot(left, right):
    return lax.dot_general(
        left, right, (((0,), (0,)), ((), ())), preferred_element_type=jnp.float32
    )


def back_dot(grad_in, weight):
    return lax.dot_general(
        grad_in, weight, (((1,), (1,)), ((), ())), preferred_element_type=jnp.float32
    )


def scores_of(query_pair, key_pair, key_mask, factor):
    raw_scores = (
        jnp.einsum("bqgd,bkgd->bgqk", query_pair, key_pair, preferred_element_type=jnp.float32)
        * factor
    )
    return jnp.where(key_mask[:, None, None, :], raw_scores, -1000000000.0)


def per_device(
    tokens,
    lengths,
    time_embed,
    cotangent,
    time_weight,
    attn_gain,
    attn_shift,
    qkv_weight,
    out_weight,
    mlp_gain,
    mlp_shift,
    up_weight,
    up_bias,
    down_weight,
    down_bias,
):
    seq_count, length, features = tokens.shape
    flat_rows = seq_count * length
    pair_count = HEADS // 2
    factor = HD ** (-0.5)
    time_full, gain_one, shift_one, qkv_full, out_full = (
        lax.all_gather(time_weight, "fsdp", axis=0, tiled=True),
        lax.all_gather(attn_gain, "fsdp", axis=0, tiled=True),
        lax.all_gather(attn_shift, "fsdp", axis=0, tiled=True),
        lax.all_gather(qkv_weight, "fsdp", axis=0, tiled=True),
        lax.all_gather(out_weight, "fsdp", axis=0, tiled=True),
    )
    gain_two, shift_two, up_full, up_bias_full, down_full, down_bias_full = (
        lax.all_gather(mlp_gain, "fsdp", axis=0, tiled=True),
        lax.all_gather(mlp_shift, "fsdp", axis=0, tiled=True),
        lax.all_gather(up_weight, "fsdp", axis=0, tiled=True),
        lax.all_gather(up_bias, "fsdp", axis=0, tiled=True),
        lax.all_gather(down_weight, "fsdp", axis=0, tiled=True),
        lax.all_gather(down_bias, "fsdp", axis=0, tiled=True),
    )
    key_mask = jnp.arange(length, dtype=jnp.int32)[None, :] < lengths[:, None]
    residual = tokens.astype(jnp.float32)
    time_scale = (
        1.0 + jnp.dot(time_embed, time_full, preferred_element_type=jnp.float32)[:, None, :]
    )
    normed_one, inverse_one = normalize(residual)
    affine_one = normed_one * gain_one.astype(jnp.float32) + shift_one.astype(jnp.float32)
    attn_in = (affine_one * time_scale).astype(jnp.bfloat16).reshape(flat_rows, features)
    qkv = jnp.dot(attn_in, qkv_full, preferred_element_type=jnp.float32).reshape(
        seq_count, length, 3, HEADS, HD
    )
    cosine_table, sine_table = rotary_tables(length, HD)
    query_rows = rotate(qkv[:, :, 0], cosine_table, sine_table).astype(jnp.bfloat16)
    key_rows = rotate(qkv[:, :, 1], cosine_table, sine_table).astype(jnp.bfloat16)
    value_rows = qkv[:, :, 2].astype(jnp.bfloat16)

    def by_pairs(values_in):
        return values_in.reshape(seq_count, length, pair_count, 2, HD).transpose(2, 0, 1, 3, 4)

    def from_pairs(values_in):
        return values_in.transpose(1, 2, 0, 3, 4).reshape(seq_count, length, features)

    query_group = by_pairs(query_rows)
    key_group = by_pairs(key_rows)
    value_group = by_pairs(value_rows)

    def attend(operands):
        query_pair, key_pair, value_pair = operands
        scores = scores_of(query_pair, key_pair, key_mask, factor)
        row_max = jnp.max(scores, axis=-1, keepdims=True)
        exponent = jnp.exp(scores - row_max)
        row_total = jnp.sum(exponent, axis=-1, keepdims=True)
        attn_probs = (exponent / row_total).astype(jnp.bfloat16)
        mixed_rows = jnp.einsum(
            "bgqk,bkgd->bqgd", attn_probs, value_pair, preferred_element_type=jnp.float32
        )
        return (mixed_rows.astype(jnp.bfloat16), (row_max + jnp.log(row_total))[..., 0])

    context_group, log_totals = lax.map(attend, (query_group, key_group, value_group))
    context = from_pairs(context_group).reshape(flat_rows, features)
    hidden = residual + jnp.dot(context, out_full, preferred_element_type=jnp.float32).reshape(
        seq_count, length, features
    )
    normed_two, inverse_two = normalize(hidden)
    affine_two = normed_two * gain_two.astype(jnp.float32) + shift_two.astype(jnp.float32)
    mlp_in = (affine_two * time_scale).astype(jnp.bfloat16).reshape(flat_rows, features)
    pre_act = jnp.dot(mlp_in, up_full, preferred_element_type=jnp.float32) + up_bias_full.astype(
        jnp.float32
    )
    active = jax.nn.gelu(pre_act).astype(jnp.bfloat16)
    branch_out = jnp.dot(
        active, down_full, preferred_element_type=jnp.float32
    ) + down_bias_full.astype(jnp.float32)
    layer_out = (hidden + branch_out.reshape(seq_count, length, features)).astype(jnp.bfloat16)
    gain_two, shift_two, up_full, up_bias_full, down_full, down_bias_full = (
        lax.all_gather(mlp_gain, "fsdp", axis=0, tiled=True),
        lax.all_gather(mlp_shift, "fsdp", axis=0, tiled=True),
        lax.all_gather(up_weight, "fsdp", axis=0, tiled=True),
        lax.all_gather(up_bias, "fsdp", axis=0, tiled=True),
        lax.all_gather(down_weight, "fsdp", axis=0, tiled=True),
        lax.all_gather(down_bias, "fsdp", axis=0, tiled=True),
    )
    grad_out = cotangent.astype(jnp.float32) * key_mask[:, :, None].astype(jnp.float32)
    grad_branch = grad_out.astype(jnp.bfloat16).reshape(flat_rows, features)
    down_weight_grad = rows_dot(active, grad_branch)
    down_bias_grad = jnp.sum(grad_branch.astype(jnp.float32), axis=0)
    grad_active = back_dot(grad_branch, down_full)
    gelu_value, gelu_pull = jax.vjp(jax.nn.gelu, pre_act)
    grad_pre = gelu_pull(grad_active)[0].astype(jnp.bfloat16)
    up_bias_grad = jnp.sum(grad_pre.astype(jnp.float32), axis=0)
    up_weight_grad = rows_dot(mlp_in, grad_pre)
    grad_mlp_in = back_dot(grad_pre, up_full).reshape(seq_count, length, features)
    grad_affine_two = grad_mlp_in * time_scale
    grad_scale = jnp.sum(grad_mlp_in * affine_two, axis=1)
    mlp_gain_grad = jnp.sum(grad_affine_two * normed_two, axis=(0, 1))
    mlp_shift_grad = jnp.sum(grad_affine_two, axis=(0, 1))
    grad_hidden = grad_out + norm_back(
        grad_affine_two * gain_two.astype(jnp.float32), normed_two, inverse_two
    )
    time_full, gain_one, shift_one, qkv_full, out_full = (
        lax.all_gather(time_weight, "fsdp", axis=0, tiled=True),
        lax.all_gather(attn_gain, "fsdp", axis=0, tiled=True),
        lax.all_gather(attn_shift, "fsdp", axis=0, tiled=True),
        lax.all_gather(qkv_weight, "fsdp", axis=0, tiled=True),
        lax.all_gather(out_weight, "fsdp", axis=0, tiled=True),
    )
    grad_attn = grad_hidden.astype(jnp.bfloat16).reshape(flat_rows, features)
    out_weight_grad = rows_dot(context, grad_attn)
    grad_context = back_dot(grad_attn, out_full).astype(jnp.bfloat16)

    def attend_back(operands):
        query_pair, key_pair, value_pair, log_pair, grad_pair = operands
        scores = scores_of(query_pair, key_pair, key_mask, factor)
        probs_full = jnp.exp(scores - log_pair[..., None])
        attn_probs = probs_full.astype(jnp.bfloat16)
        grad_value = jnp.einsum(
            "bgqk,bqgd->bkgd", attn_probs, grad_pair, preferred_element_type=jnp.float32
        )
        grad_probs = jnp.einsum(
            "bqgd,bkgd->bgqk", grad_pair, value_pair, preferred_element_type=jnp.float32
        )
        grad_scores = probs_full * (
            grad_probs - jnp.sum(grad_probs * probs_full, axis=-1, keepdims=True)
        )
        grad_scores = grad_scores.astype(jnp.bfloat16)
        grad_query = (
            jnp.einsum("bgqk,bkgd->bqgd", grad_scores, key_pair, preferred_element_type=jnp.float32)
            * factor
        )
        grad_key = (
            jnp.einsum(
                "bgqk,bqgd->bkgd", grad_scores, query_pair, preferred_element_type=jnp.float32
            )
            * factor
        )
        return (grad_query, grad_key, grad_value)

    grad_query_group, grad_key_group, grad_value_group = lax.map(
        attend_back, (query_group, key_group, value_group, log_totals, by_pairs(grad_context))
    )
    head_shape = (seq_count, length, HEADS, HD)
    grad_query_raw = rotate_back(
        from_pairs(grad_query_group).reshape(head_shape), cosine_table, sine_table
    )
    grad_key_raw = rotate_back(
        from_pairs(grad_key_group).reshape(head_shape), cosine_table, sine_table
    )
    grad_value_raw = from_pairs(grad_value_group).reshape(head_shape)
    grad_qkv = (
        jnp.stack([grad_query_raw, grad_key_raw, grad_value_raw], axis=2)
        .astype(jnp.bfloat16)
        .reshape(flat_rows, 3 * features)
    )
    qkv_weight_grad = rows_dot(attn_in, grad_qkv)
    grad_attn_in = back_dot(grad_qkv, qkv_full).reshape(seq_count, length, features)
    grad_affine_one = grad_attn_in * time_scale
    grad_scale = grad_scale + jnp.sum(grad_attn_in * affine_one, axis=1)
    attn_gain_grad = jnp.sum(grad_affine_one * normed_one, axis=(0, 1))
    attn_shift_grad = jnp.sum(grad_affine_one, axis=(0, 1))
    token_grad = (
        grad_hidden
        + norm_back(grad_affine_one * gain_one.astype(jnp.float32), normed_one, inverse_one)
    ).astype(jnp.bfloat16)
    time_weight_grad = jnp.dot(
        time_embed.astype(jnp.float32).T, grad_scale, precision=lax.Precision.HIGHEST
    )
    parts_all = (
        lax.psum_scatter(
            time_weight_grad.astype(jnp.bfloat16), "fsdp", scatter_dimension=0, tiled=True
        ).astype(jnp.float32),
        lax.psum_scatter(
            attn_gain_grad.astype(jnp.bfloat16), "fsdp", scatter_dimension=0, tiled=True
        ).astype(jnp.float32),
        lax.psum_scatter(
            attn_shift_grad.astype(jnp.bfloat16), "fsdp", scatter_dimension=0, tiled=True
        ).astype(jnp.float32),
        lax.psum_scatter(
            qkv_weight_grad.astype(jnp.bfloat16), "fsdp", scatter_dimension=0, tiled=True
        ).astype(jnp.float32),
        lax.psum_scatter(
            out_weight_grad.astype(jnp.bfloat16), "fsdp", scatter_dimension=0, tiled=True
        ).astype(jnp.float32),
        lax.psum_scatter(
            mlp_gain_grad.astype(jnp.bfloat16), "fsdp", scatter_dimension=0, tiled=True
        ).astype(jnp.float32),
        lax.psum_scatter(
            mlp_shift_grad.astype(jnp.bfloat16), "fsdp", scatter_dimension=0, tiled=True
        ).astype(jnp.float32),
        lax.psum_scatter(
            up_weight_grad.astype(jnp.bfloat16), "fsdp", scatter_dimension=0, tiled=True
        ).astype(jnp.float32),
        lax.psum_scatter(
            up_bias_grad.astype(jnp.bfloat16), "fsdp", scatter_dimension=0, tiled=True
        ).astype(jnp.float32),
        lax.psum_scatter(
            down_weight_grad.astype(jnp.bfloat16), "fsdp", scatter_dimension=0, tiled=True
        ).astype(jnp.float32),
        lax.psum_scatter(
            down_bias_grad.astype(jnp.bfloat16), "fsdp", scatter_dimension=0, tiled=True
        ).astype(jnp.float32),
    )
    attn_parts = parts_all[:5]
    mlp_parts = parts_all[5:]
    summed = (
        lax.psum(attn_parts[0].astype(jnp.bfloat16), "dp").astype(jnp.float32),
        lax.psum(attn_parts[1].astype(jnp.bfloat16), "dp").astype(jnp.float32),
        lax.psum(attn_parts[2].astype(jnp.bfloat16), "dp").astype(jnp.float32),
        lax.psum(attn_parts[3].astype(jnp.bfloat16), "dp").astype(jnp.float32),
        lax.psum(attn_parts[4].astype(jnp.bfloat16), "dp").astype(jnp.float32),
        lax.psum(mlp_parts[0].astype(jnp.bfloat16), "dp").astype(jnp.float32),
        lax.psum(mlp_parts[1].astype(jnp.bfloat16), "dp").astype(jnp.float32),
        lax.psum(mlp_parts[2].astype(jnp.bfloat16), "dp").astype(jnp.float32),
        lax.psum(mlp_parts[3].astype(jnp.bfloat16), "dp").astype(jnp.float32),
        lax.psum(mlp_parts[4].astype(jnp.bfloat16), "dp").astype(jnp.float32),
        lax.psum(mlp_parts[5].astype(jnp.bfloat16), "dp").astype(jnp.float32),
    )
    return (
        layer_out,
        token_grad,
        summed[0],
        summed[1],
        summed[2],
        summed[3],
        summed[4],
        summed[5],
        summed[6],
        summed[7],
        summed[8],
        summed[9],
        summed[10],
    )


def solution(mesh):
    return jax.shard_map(
        per_device,
        mesh=mesh,
        in_specs=(
            P(("dp", "fsdp"), None, None),
            P(("dp", "fsdp")),
            P(("dp", "fsdp"), None),
            P(("dp", "fsdp"), None, None),
            P("fsdp", None),
            P("fsdp"),
            P("fsdp"),
            P("fsdp", None),
            P("fsdp", None),
            P("fsdp"),
            P("fsdp"),
            P("fsdp", None),
            P("fsdp"),
            P("fsdp", None),
            P("fsdp"),
        ),
        out_specs=(
            P(("dp", "fsdp"), None, None),
            P(("dp", "fsdp"), None, None),
            P("fsdp", None),
            P("fsdp"),
            P("fsdp"),
            P("fsdp", None),
            P("fsdp", None),
            P("fsdp"),
            P("fsdp"),
            P("fsdp", None),
            P("fsdp"),
            P("fsdp", None),
            P("fsdp"),
        ),
        check_vma=False,
    )
```

profile of v0, /device:TPU:0, one launch (start us, length us, event | category | flops | bytes accessed | tf_op | source)
XLA Modules:
  0.0 823.5 jit_solution(15790023884834420819)
XLA Ops:
  15.5 37.3 %all-reduce.12 = (bf16[1024]{0:T(1024)(128)(2,1)S(1)}, bf16[1024]{0:T(1024)(128)(2,1)S(1)}, bf16[1024]{0:T(1024)(128)(2,1)S(1)}, bf16[1024]{0:T(1024)(128)(2,1)S(1)}) all-reduce(bf16[1024]{0:T(1024)(128)(2,1)S(1)} %dynamic-update-slice.1, bf16[1024]{0:T(1024)(128)(2,1)S(1)} %dynamic-update-slice, ...), channel_id=1, replica_groups=mesh['dp'=2,'fsdp'=16] {'fsdp'}, use_global_device_ids=true, to_apply=%add.1 | all-reduce | flops 4096 | bytes 16384
  53.6 17.7 %all-gather = bf16[16,1,256]{2,1,0:T(2,128)(2,1)S(1)} all-gather(bf16[1,1,256]{2,1,0:T(2,128)(2,1)S(1)} %reshape.823), channel_id=1, replica_groups=mesh['dp'=2,'fsdp'=16] {'fsdp'}, dimensions={0}, use_global_device_ids=true | all-gather | bytes 8704 | tf_op jit(solution)/shard_map/all_gather | solution.py:101
  72.9 21.5 %all_gather.41 = bf16[256,1024]{1,0:T(8,128)(2,1)S(1)} all-gather(bf16[16,1024]{1,0:T(8,128)(2,1)S(1)} %copy-done.9), channel_id=1, replica_groups=mesh['dp'=2,'fsdp'=16] {'fsdp'}, dimensions={0}, use_global_device_ids=true | all-gather | bytes 557056 | tf_op jit(solution)/shard_map/all_gather | solution.py:91
  94.6 8.6 %copy.59 = bf16[3072,1024]{1,0:T(8,128)(2,1)} copy(bf16[3072,1024]{0,1:T(8,128)(2,1)} %bitcast.284) | data formatting | bytes 12582912 | tf_op jit(solution)/shard_map/dot_general | solution.py:113
  103.2 6.4 convolution_bitcast_fusion.1
  112.3 2.5 fusion.89
  114.8 39.9 %while.28 = (s32[]{:T(128)}, bf16[8,1,512,2,64]{2,4,3,1,0:T(8,128)(2,1)}, f32[8,1,2,512]{3,2,1,0:T(2,128)S(1)}, bf16[8,1,512,2,64]{2,4,3,1,0:T(8,128)(2,1)}, bf1...) while((s32[]{:T(128)}, ...), condition=%wide.region_5.6_spmd.clone, body=%wide.region_2.5_spmd.clone.sunk | while | flops 140574208 | bytes 6852709 | solution.py:143
  127.5 2.3 fusion.159
  152.4 2.3 fusion.159
  154.8 3.3 fusion.122
  158.4 34.5 %all-gather.10.cloned.1.call-done = bf16[1024,4096]{1,0:T(8,128)(2,1)} async-done(((bf16[64,4096]{1,0:T(8,128)(2,1)}), bf16[1024,4096]{1,0:T(8,128)(2,1)}) %all-gather.10.cloned.1.call-update) | async-done | bytes 8388624 | tf_op jit(solution)/shard_map/all_gather | solution.py:100
  193.0 10.3 %fusion.118 = f32[512,4096]{1,0:T(8,128)} fusion(bf16[1024,4096]{1,0:T(8,128)(2,1)} %all-gather.10.cloned.1.call-done, f32[1,512,1024]{2,1,0:T(8,128)S(1)} %get-tuple-element.271, f32[1024]{0:T(1024)S(1)} %convert_element_type.239, f32[1024]{0:T(1024)S(1)} %convert_element_type.238, f32[512]{0:T(512)S(1)} %add_rsqrt_fusion, ...), kind=kOutput, calls=%fused_computation.184 | convolution fusion | flops 4298113024 | bytes 18890752 | tf_op jit(solution)/shard_map/dot_general | solution.py:151
  203.3 64.6 %all-gather.12.cloned.1.call-done = bf16[4096,1024]{1,0:T(8,128)(2,1)} async-done(((bf16[256,1024]{1,0:T(8,128)(2,1)}), bf16[4096,1024]{1,0:T(8,128)(2,1)}) %all-gather.12.cloned.1.call-update) | async-done | bytes 8388624 | tf_op jit(solution)/shard_map/all_gather | solution.py:102
  267.9 13.6 %fusion.123 = (bf16[4096]{0:T(1024)(128)(2,1)S(1)}, bf16[512,4096]{1,0:T(8,128)(2,1)S(1)}) fusion(f32[512,4096]{1,0:T(8,128)} %fusion.118, f32[4096]{0:T(1024)S(1)} %bitcast.298, bf16[4096,1024]{1,0:T(8,128)(2,1)} %all-gather.12.cloned.1.call-done, f32[512]{0:T(512)S(1)} %fusion.109, bf16[1,512,1024]{2,1,0:T(8,128)(2,1)} %param.22), kind=kOutput, calls=%fused_computation.188 | convolution fusion | flops 4342673408 | bytes 22046720 | tf_op jit(solution)/shard_map/dot_general | solution.py:56
  281.5 5.2 fusion.79
  290.2 2.6 convolution_convert_fusion.4
  292.8 4.5 convolution_convert_fusion.5
  297.3 2.3 copy.67
  299.7 82.7 %while.29 = (s32[]{:T(128)}, f32[8,1,512,2,64]{2,4,3,1,0:T(8,128)}, f32[8,1,512,2,64]{2,4,3,1,0:T(8,128)}, bf16[8,1,512,2,64]{2,4,3,1,0:T(8,128)(2,1)}, bf16[8,1...) while((s32[]{:T(128)}, f32[8,1,512,2,64]{2,4,3,1,0:T(8,128)}, ...), condition=%wide.region_12.13_spmd.clone, body=%wide.region_10.12_spmd.clone.sunk | while | flops 340393472 | bytes 17459324 | solution.py:222
  382.4 2.9 broadcast_multiply_fusion.1
  392.6 6.1 convolution_convert_fusion.3
  398.7 9.2 %convolution_convert_fusion.2 = bf16[1024,4096]{1,0:T(8,128)(2,1)} fusion(bf16[512,4096]{1,0:T(8,128)(2,1)} %copy-done.14, f32[1,512,1024]{2,1,0:T(8,128)S(1)} %get-tuple-element.271, f32[1024]{0:T(1024)S(1)} %convert_element_type.239, f32[1024]{0:T(1024)S(1)} %convert_element_type.238, f32[512]{0:T(512)S(1)} %add_rsqrt_fusion, ...), kind=kOutput, calls=%fused_computation.69 | convolution fusion | flops 4302307328 | bytes 14696448 | tf_op jit(solution)/shard_map/dot_general | solution.py:50
  408.4 14.2 %convolution_convert_fusion.1 = bf16[4096,1024]{1,0:T(8,128)(2,1)} fusion(bf16[1,512,1024]{2,1,0:T(8,128)(2,1)} %param.22, f32[512]{0:T(512)S(1)} %fusion.109, f32[512,4096]{1,0:T(8,128)} %fusion.118, f32[4096]{0:T(1024)S(1)} %bitcast.299), kind=kOutput, calls=%fused_computation.68 | convolution fusion | flops 4321705984 | bytes 17844224 | tf_op jit(solution)/shard_map/dot_general | solution.py:50
  426.3 8.2 fusion.69
  436.3 59.9 %all-reduce.11 = (bf16[1024]{0:T(1024)(128)(2,1)S(1)}, bf16[1024]{0:T(1024)(128)(2,1)S(1)}, bf16[1024]{0:T(1024)(128)(2,1)S(1)}, bf16[1024]{0:T(1024)(128)(2,1)S...) all-reduce(bf16[1024]{0:T(1024)(128)(2,1)S(1)} %dynamic-update-slic, ...), channel_id=1, replica_groups=mesh['dp'=2,'fsdp'=16] {'fsdp'}, use_global_device_ids=true, to_apply=%add.4 | all-reduce | flops 10240 | bytes 40960
  497.8 4.4 fusion.68
  502.2 87.4 %reduce-scatter.12.cloned.1.call-done = bf16[64,4096]{1,0:T(8,128)(2,1)} async-done(((bf16[1024,4096]{1,0:T(8,128)(2,1)}), bf16[64,4096]{1,0:T(8,128)(2,1)}) %reduce-scatter.12.cloned.1.call-update) | async-done | bytes 524304 | tf_op jit(solution)/shard_map/reduce_scatter | solution.py:273
  589.6 107.2 %reduce-scatter.14.cloned.1.call-done = bf16[256,1024]{1,0:T(8,128)(2,1)} async-done(((bf16[4096,1024]{1,0:T(8,128)(2,1)}), bf16[256,1024]{1,0:T(8,128)(2,1)}) %reduce-scatter.14.cloned.1.call-update) | async-done | bytes 524304 | tf_op jit(solution)/shard_map/reduce_scatter | solution.py:279
  696.8 12.2 %fusion.84 = bf16[1,512,1024]{2,1,0:T(8,128)(2,1)} fusion(f32[1,512,1024]{2,1,0:T(8,128)S(1)} %get-tuple-element.271, bf16[4096,1024]{1,0:T(8,128)(2,1)} %all-gather.12.cloned.1.call-done, f32[1024]{0:T(1024)S(1)} %convert_element_type.243, f32[512,4096]{1,0:T(8,128)} %fusion.118, f32[4096]{0:T(1024)S(1)} %bitcast.300), kind=kOutput, calls=%fused_computation.120 | convolution fusion | flops 4317511680 | bytes 19943424 | tf_op jit(solution)/shard_map/dot_general | solution.py:155
  709.0 47.7 %reduce-scatter.6.cloned.1.call-done = bf16[16,1024]{1,0:T(8,128)(2,1)} async-done(((bf16[256,1024]{1,0:T(8,128)(2,1)}), bf16[16,1024]{1,0:T(8,128)(2,1)}) %reduce-scatter.6.cloned.1.call-update) | async-done | bytes 32784 | tf_op jit(solution)/shard_map/reduce_scatter | solution.py:252
  756.7 9.3 %all-reduce.13 = (bf16[16,1024]{1,0:T(8,128)(2,1)S(1)}, bf16[64]{0:T(256)(128)(2,1)S(1)}, bf16[64]{0:T(256)(128)(2,1)S(1)}, bf16[64]{0:T(256)(128)(2,1)S(1)}, bf...) all-reduce(bf16[16,1024]{1,0:T(8,128)(2,1)} %reduce-scatter.6.clone, ...), channel_id=1, replica_groups=mesh['dp'=2,'fsdp'=16] {'dp'}, use_global_device_ids=true, to_apply=%region_18.19 | all-reduce | flops 16960 | bytes 67840 | tf_op jit(solution)/shard_map/psum | solution.py:289
  769.8 39.9 %all-reduce.17.cloned.1.call-done = (bf16[64,3072]{1,0:T(8,128)(2,1)}, bf16[64,1024]{1,0:T(8,128)(2,1)}, bf16[64,4096]{1,0:T(8,128)(2,1)}, bf16[256,1024]{1,0:T(8,128)(2,1)}) async-done(((bf16[64,3072]{1,0:T(8,128)(2,1)}, bf16[64,1024]{1,0:T(8,128)(2,1)}, bf16[64,4096]{1,0:T(8,128)(2,1)}, bf16[256,1024]{1,0:T(8,128)(2,1)}), (bf16[64,3072]{1,0:T(8,128)(2,1)}, bf16[64,1024]{1,0:T(8,128)(2,1)}, ...) | async-done | bytes 1572880 | tf_op jit(solution)/shard_map/psum | solution.py:292
  (229 shorter events, 157.4 us)
Async XLA Ops:
  7.2 65.0 %copy-start.2 = (bf16[1,512,1024]{2,1,0:T(8,128)(2,1)S(1)}, bf16[1,512,1024]{2,1,0:T(8,128)(2,1)}, u32[]{:S(2)}) copy-start(bf16[1,512,1024]{2,1,0:T(8,128)(2,1)} %param.19) | copy-start | bytes 3145732
  7.2 65.7 %copy-start.9 = (bf16[16,1024]{1,0:T(8,128)(2,1)S(1)}, bf16[16,1024]{1,0:T(8,128)(2,1)}, u32[]{:S(2)}) copy-start(bf16[16,1024]{1,0:T(8,128)(2,1)} %param.23) | copy-start | bytes 98308
  7.2 87.4 %all-gather.6.cloned.1.call-start = ((), (), s32[]{:S(2)}) async-start(), calls=%async_computation.5 | async-start | bytes 6684672 | tf_op jit(solution)/shard_map/all_gather | solution.py:94
  7.9 146.9 %all-gather.8.cloned.1.call-start = ((), (), s32[]{:S(2)}) async-start(), calls=%async_computation.6 | async-start | bytes 2228224 | tf_op jit(solution)/shard_map/all_gather | solution.py:95
  8.7 85.7 %copy-start.10 = (bf16[1,256]{1,0:T(2,128)(2,1)S(1)}, bf16[1,256]{1,0:T(2,128)(2,1)}, u32[]{:S(2)}) copy-start(bf16[1,256]{1,0:T(2,128)(2,1)} %param.21) | copy-start | bytes 1540
  8.7 184.3 %all-gather.10.cloned.1.call-start = ((), (), s32[]{:S(2)}) async-start(), calls=%async_computation.7 | async-start | bytes 8912896 | tf_op jit(solution)/shard_map/all_gather | solution.py:100
  9.4 258.5 %all-gather.12.cloned.1.call-start = ((), (), s32[]{:S(2)}) async-start(), calls=%async_computation.8 | async-start | bytes 8912896 | tf_op jit(solution)/shard_map/all_gather | solution.py:102
  10.0 492.2 %reduce-scatter.10.cloned.1.call-start = ((), (), s32[]{:S(2)}) async-start(), calls=%async_computation.11 | async-start | bytes 2228224 | tf_op jit(solution)/shard_map/reduce_scatter | solution.py:264
  267.9 13.7 %copy-start.12 = (bf16[1024,4096]{1,0:T(8,128)(2,1)S(1)}, bf16[1024,4096]{1,0:T(8,128)(2,1)}, u32[]{:S(2)}) copy-start(bf16[1024,4096]{1,0:T(8,128)(2,1)} %all-gather.10.cloned.1.call-done) | copy-start | bytes 25165828
  281.5 5.2 copy-start.14
  286.8 1.2 copy-start.5
  288.0 2.2 copy-start.6
  288.9 1.3 copy-start.4
  299.6 202.6 %reduce-scatter.8.cloned.1.call-start = ((), (), s32[]{:S(2)}) async-start(), calls=%async_computation.10 | async-start | bytes 6684672 | tf_op jit(solution)/shard_map/reduce_scatter | solution.py:261
  385.9 1.6 copy-start
  385.9 2.2 copy-start.1
  389.3 1.2 copy-start.7
  398.7 190.9 %reduce-scatter.12.cloned.1.call-start = ((), (), s32[]{:S(2)}) async-start(), calls=%async_computation.12 | async-start | bytes 8912896 | tf_op jit(solution)/shard_map/reduce_scatter | solution.py:273
  408.0 288.8 %reduce-scatter.14.cloned.1.call-start = ((), (), s32[]{:S(2)}) async-start(), calls=%async_computation.13 | async-start | bytes 8912896 | tf_op jit(solution)/shard_map/reduce_scatter | solution.py:279
  422.6 0.7 copy-start.11
  422.6 2.0 copy-start.13
  422.6 334.1 %reduce-scatter.6.cloned.1.call-start = ((), (), s32[]{:S(2)}) async-start(), calls=%async_computation.9 | async-start | bytes 557056 | tf_op jit(solution)/shard_map/reduce_scatter | solution.py:252
  434.6 1.4 copy-start.3
  497.5 312.2 %all-reduce.17.cloned.1.call-start = ((), (), s32[]{:S(2)}) async-start(), calls=%async_computation.14 | async-start | bytes 3145728 | tf_op jit(solution)/shard_map/psum | solution.py:292
  809.7 5.7 copy-start.8
Sparse Core Ops, SparseCore 0:
  10.3 64.5 all-gather.5
  77.0 40.6 all-gather.7
  119.9 73.0 all-gather.9
  195.0 72.8 all-gather.11
  299.7 60.4 reduce-scatter.9
  398.8 84.3 reduce-scatter.7
  487.3 102.2 reduce-scatter.11
  593.6 103.0 reduce-scatter.13
  700.9 55.8 reduce-scatter.5
  759.1 50.5 all-reduce.16
where the time goes:
time: 828 us; the launch traced here: 824 us
  waiting for transfers between devices  384 us (46%)
  matrix products  199 us (24%)
  blocking collectives  146 us (18%)
  other arithmetic  51.4 us (6%)
  local copies, waits for them, and re-layouts  24.6 us (3%)
  between operations  17.4 us (2%)
    reduce_scatter x1, waiting for transfers between devices, per_device(): lax.psum_scatter(down_weight_grad.astype(jnp.bfloat16), 'fsdp', scatter_d...  107 us
    unnamed x2, blocking collectives  97.2 us
    reduce_scatter x1, waiting for transfers between devices, per_device(): lax.psum_scatter(up_weight_grad.astype(jnp.bfloat16), 'fsdp', scatter_dim...  87.4 us
    all_gather x1, waiting for transfers between devices, per_device(): lax.all_gather(down_weight, 'fsdp', axis=0, tiled=True)  64.6 us
    reduce_scatter x1, waiting for transfers between devices, per_device(): lax.psum_scatter(time_weight_grad.astype(jnp.bfloat16), 'fsdp', scatter_d...  47.7 us
    psum x1, waiting for transfers between devices, per_device(): lax.psum(attn_parts[3].astype(jnp.bfloat16), 'dp').astype(jnp.float32)  39.9 us
    all_gather x1, waiting for transfers between devices, per_device(): lax.all_gather(up_weight, 'fsdp', axis=0, tiled=True)  34.5 us
    dot_general x4, matrix products, rows_dot(): lax.dot_general(left, right, (((0,), (0,)), ((), ())), preferred_element_...  32 us
  transfers between devices with their start and end apart: 10, of which 6 were waited for; matrix products, arithmetic and copies ran while one was open for 28% of the time, Pallas kernels for 0%

commit v1 on v0

--- a/solution.py
+++ b/solution.py
@@ -6,6 +6,11 @@
 
 HEADS = 16
 HD = 64
+
+
+def gather_and_add(block, mesh_axis):
+    pieces = lax.all_gather(block, mesh_axis)
+    return jnp.sum(pieces, axis=0)
 
 
 def normalize(values_in):
@@ -289,7 +294,7 @@
         lax.psum(attn_parts[0].astype(jnp.bfloat16), "dp").astype(jnp.float32),
         lax.psum(attn_parts[1].astype(jnp.bfloat16), "dp").astype(jnp.float32),
         lax.psum(attn_parts[2].astype(jnp.bfloat16), "dp").astype(jnp.float32),
-        lax.psum(attn_parts[3].astype(jnp.bfloat16), "dp").astype(jnp.float32),
+        gather_and_add(attn_parts[3].astype(jnp.bfloat16), "dp").astype(jnp.float32),
         lax.psum(attn_parts[4].astype(jnp.bfloat16), "dp").astype(jnp.float32),
         lax.psum(mlp_parts[0].astype(jnp.bfloat16), "dp").astype(jnp.float32),
         lax.psum(mlp_parts[1].astype(jnp.bfloat16), "dp").astype(jnp.float32),

time: 828 us -> 778 us (0.940)
  waiting for transfers between devices: 384 us -> 328 us
  blocking collectives: 146 us -> 162 us
    reduce_scatter x1, waiting for transfers between devices: 87.4 us -> 0.01 us  [per_device(): lax.psum_scatter(up_weight_grad.astype(jnp.bfloat16), 'fsdp', scatter_dim...]
    reduce_scatter x1, waiting for transfers between devices: 0.01 us -> 75.2 us  [per_device(): lax.psum_scatter(qkv_weight_grad.astype(jnp.bfloat16), 'fsdp', scatter_di...]
    reduce_scatter x1, waiting for transfers between devices: 107 us -> 68.9 us  [per_device(): lax.psum_scatter(down_weight_grad.astype(jnp.bfloat16), 'fsdp', scatter_d...]
    all_gather x0 -> x1, blocking collectives: none -> 15.3 us  [gather_and_add(): pieces = lax.all_gather(block, mesh_axis)]
    psum x1, waiting for transfers between devices: 39.9 us -> 29.7 us  [per_device(): lax.psum(attn_parts[4].astype(jnp.bfloat16), 'dp').astype(jnp.float32)]
  transfers between devices with their start and end apart: 10 -> 10, of which waited for: 6 -> 6; matrix products, arithmetic and copies ran while one was open for 28% -> 30% of each run, Pallas kernels for 0% -> 0%
where the time goes in v1:
time: 778 us; the launch traced here: 773 us
  waiting for transfers between devices  328 us (42%)
  matrix products  191 us (25%)
  blocking collectives  162 us (21%)
  other arithmetic  48.4 us (6%)
  local copies, waits for them, and re-layouts  25.9 us (3%)
  between operations  17.4 us (2%)
    unnamed x2, blocking collectives  97.8 us
    reduce_scatter x1, waiting for transfers between devices, per_device(): lax.psum_scatter(qkv_weight_grad.astype(jnp.bfloat16), 'fsdp', scatter_di...  75.2 us
    reduce_scatter x1, waiting for transfers between devices, per_device(): lax.psum_scatter(down_weight_grad.astype(jnp.bfloat16), 'fsdp', scatter_d...  68.9 us
    all_gather x1, waiting for transfers between devices, per_device(): lax.all_gather(down_weight, 'fsdp', axis=0, tiled=True)  64.6 us
    reduce_scatter x1, waiting for transfers between devices, per_device(): lax.psum_scatter(time_weight_grad.astype(jnp.bfloat16), 'fsdp', scatter_d...  45.3 us
    all_gather x1, waiting for transfers between devices, per_device(): lax.all_gather(up_weight, 'fsdp', axis=0, tiled=True)  41.6 us
    dot_general x4, matrix products, rows_dot(): lax.dot_general(left, right, (((0,), (0,)), ((), ())), preferred_element_...  33.7 us
    psum x1, waiting for transfers between devices, per_device(): lax.psum(attn_parts[4].astype(jnp.bfloat16), 'dp').astype(jnp.float32)  29.7 us
  transfers between devices with their start and end apart: 10, of which 6 were waited for; matrix products, arithmetic and copies ran while one was open for 30% of the time, Pallas kernels for 0%

profile of v1, /device:TPU:0, one launch (start us, length us, event | category | flops | bytes accessed | tf_op | source)
XLA Modules:
  0.0 773.3 jit_solution(15781430290801108633)
XLA Ops:
  15.5 37.3 %all-reduce.12 = (bf16[1024]{0:T(1024)(128)(2,1)S(1)}, bf16[1024]{0:T(1024)(128)(2,1)S(1)}, bf16[1024]{0:T(1024)(128)(2,1)S(1)}, bf16[1024]{0:T(1024)(128)(2,1)S(1)}) all-reduce(bf16[1024]{0:T(1024)(128)(2,1)S(1)} %dynamic-update-slice.1, bf16[1024]{0:T(1024)(128)(2,1)S(1)} %dynamic-update-slice, ...), channel_id=1, replica_groups=mesh['dp'=2,'fsdp'=16] {'fsdp'}, use_global_device_ids=true, to_apply=%add.1 | all-reduce | flops 4096 | bytes 16384
  53.5 17.8 %all-gather.1 = bf16[16,1,256]{2,1,0:T(2,128)(2,1)S(1)} all-gather(bf16[1,1,256]{2,1,0:T(2,128)(2,1)S(1)} %reshape.824), channel_id=1, replica_groups=mesh['dp'=2,'fsdp'=16] {'fsdp'}, dimensions={0}, use_global_device_ids=true | all-gather | bytes 8704 | tf_op jit(solution)/shard_map/all_gather | solution.py:106
  72.9 21.8 %all_gather.47 = bf16[256,1024]{1,0:T(8,128)(2,1)S(1)} all-gather(bf16[16,1024]{1,0:T(8,128)(2,1)S(1)} %copy-done.12), channel_id=1, replica_groups=mesh['dp'=2,'fsdp'=16] {'fsdp'}, dimensions={0}, use_global_device_ids=true | all-gather | bytes 557056 | tf_op jit(solution)/shard_map/all_gather | solution.py:96
  94.9 8.6 %copy.59 = bf16[3072,1024]{1,0:T(8,128)(2,1)} copy(bf16[3072,1024]{0,1:T(8,128)(2,1)} %bitcast.285) | data formatting | bytes 12582912 | tf_op jit(solution)/shard_map/dot_general | solution.py:118
  103.5 6.4 convolution_bitcast_fusion.1
  114.1 32.2 %while.28 = (s32[]{:T(128)}, bf16[8,1,512,2,64]{2,4,3,1,0:T(8,128)(2,1)}, f32[8,1,2,512]{3,2,1,0:T(2,128)S(1)}, bf16[8,1,512,2,64]{2,4,3,1,0:T(8,128)(2,1)}, bf1...) while((s32[]{:T(128)}, ...), condition=%wide.region_5.6_spmd.clone, body=%wide.region_2.5_spmd.clone.sunk | while | flops 140574208 | bytes 6852709 | solution.py:148
  115.8 2.3 fusion.159
  136.0 2.3 fusion.159
  140.0 2.3 fusion.159
  144.0 2.3 fusion.159
  147.7 3.3 fusion.122
  151.3 41.6 %all-gather.11.cloned.1.call-done = bf16[1024,4096]{1,0:T(8,128)(2,1)} async-done(((bf16[64,4096]{1,0:T(8,128)(2,1)}), bf16[1024,4096]{1,0:T(8,128)(2,1)}) %all-gather.11.cloned.1.call-update) | async-done | bytes 8388624 | tf_op jit(solution)/shard_map/all_gather | solution.py:105
  192.9 10.3 %fusion.118 = f32[512,4096]{1,0:T(8,128)} fusion(bf16[1024,4096]{1,0:T(8,128)(2,1)} %all-gather.11.cloned.1.call-done, f32[1,512,1024]{2,1,0:T(8,128)S(1)} %get-tuple-element.270, f32[1024]{0:T(1024)S(1)} %convert_element_type.241, f32[1024]{0:T(1024)S(1)} %convert_element_type.240, f32[512]{0:T(512)S(1)} %add_rsqrt_fusion, ...), kind=kOutput, calls=%fused_computation.184 | convolution fusion | flops 4298113024 | bytes 18890752 | tf_op jit(solution)/shard_map/dot_general | solution.py:156
  203.2 64.6 %all-gather.13.cloned.1.call-done = bf16[4096,1024]{1,0:T(8,128)(2,1)} async-done(((bf16[256,1024]{1,0:T(8,128)(2,1)}), bf16[4096,1024]{1,0:T(8,128)(2,1)}) %all-gather.13.cloned.1.call-update) | async-done | bytes 8388624 | tf_op jit(solution)/shard_map/all_gather | solution.py:107
  267.9 13.6 %fusion.123 = (bf16[4096]{0:T(1024)(128)(2,1)S(1)}, bf16[512,4096]{1,0:T(8,128)(2,1)S(1)}) fusion(f32[512,4096]{1,0:T(8,128)} %fusion.118, f32[4096]{0:T(1024)S(1)} %bitcast.302, bf16[4096,1024]{1,0:T(8,128)(2,1)} %all-gather.13.cloned.1.call-done, f32[512]{0:T(512)S(1)} %fusion.109, bf16[1,512,1024]{2,1,0:T(8,128)(2,1)} %param.22), kind=kOutput, calls=%fused_computation.188 | convolution fusion | flops 4342673408 | bytes 22046720 | tf_op jit(solution)/shard_map/dot_general | solution.py:61
  281.5 5.2 fusion.79
  290.3 2.6 convolution_convert_fusion.4
  292.9 9.4 %convolution_convert_fusion.2 = bf16[1024,4096]{1,0:T(8,128)(2,1)} fusion(bf16[512,4096]{1,0:T(8,128)(2,1)} %copy-done.16, f32[1,512,1024]{2,1,0:T(8,128)S(1)} %get-tuple-element.270, f32[1024]{0:T(1024)S(1)} %convert_element_type.241, f32[1024]{0:T(1024)S(1)} %convert_element_type.240, f32[512]{0:T(512)S(1)} %add_rsqrt_fusion, ...), kind=kOutput, calls=%fused_computation.69 | convolution fusion | flops 4302307328 | bytes 14696448 | tf_op jit(solution)/shard_map/dot_general | solution.py:55
  302.5 4.6 convolution_convert_fusion.5
  309.3 13.6 %convolution_convert_fusion.1 = bf16[4096,1024]{1,0:T(8,128)(2,1)} fusion(bf16[1,512,1024]{2,1,0:T(8,128)(2,1)} %param.22, f32[512]{0:T(512)S(1)} %fusion.109, f32[512,4096]{1,0:T(8,128)} %fusion.118, f32[4096]{0:T(1024)S(1)} %bitcast.303), kind=kOutput, calls=%fused_computation.68 | convolution fusion | flops 4321705984 | bytes 17844224 | tf_op jit(solution)/shard_map/dot_general | solution.py:55
  323.0 83.2 %while.29 = (s32[]{:T(128)}, f32[8,1,512,2,64]{2,4,3,1,0:T(8,128)}, f32[8,1,512,2,64]{2,4,3,1,0:T(8,128)}, bf16[8,1,512,2,64]{2,4,3,1,0:T(8,128)(2,1)}, bf16[8,1...) while((s32[]{:T(128)}, f32[8,1,512,2,64]{2,4,3,1,0:T(8,128)}, ...), condition=%wide.region_12.13_spmd.clone, body=%wide.region_10.12_spmd.clone.sunk | while | flops 340393472 | bytes 17459324 | solution.py:227
  406.1 3.0 broadcast_multiply_fusion.1
  417.9 5.6 fusion.69
  424.4 8.1 %convolution_convert_fusion.3 = bf16[1024,3072]{1,0:T(8,128)(2,1)} fusion(bf16[512,3072]{0,1:T(8,128)(2,1)} %bitcast.295, bf16[1,512,1024]{2,1,0:T(8,128)(2,1)S(1)} %copy-done.2, f32[1024]{0:T(1024)S(1)} %broadcast_add_fusion, f32[1024]{0:T(1024)S(1)} %convert_element_type.235, f32[1024]{0:T(1024)S(1)} %convert_element_type.234, ...), kind=kOutput, calls=%fused_computation.70 | convolution fusion | flops 3228041216 | bytes 10502144 | tf_op jit(solution)/shard_map/dot_general | solution.py:55
  437.7 60.6 %all-reduce.11 = (bf16[1024]{0:T(1024)(128)(2,1)S(1)}, bf16[1024]{0:T(1024)(128)(2,1)S(1)}, bf16[1024]{0:T(1024)(128)(2,1)S(1)}, bf16[1024]{0:T(1024)(128)(2,1)S...) all-reduce(bf16[1024]{0:T(1024)(128)(2,1)S(1)} %dynamic-update-slic, ...), channel_id=1, replica_groups=mesh['dp'=2,'fsdp'=16] {'fsdp'}, use_global_device_ids=true, to_apply=%add.4 | all-reduce | flops 10240 | bytes 40960
  498.3 68.9 %reduce-scatter.14.cloned.1.call-done = bf16[256,1024]{1,0:T(8,128)(2,1)} async-done(((bf16[4096,1024]{1,0:T(8,128)(2,1)}), bf16[256,1024]{1,0:T(8,128)(2,1)}) %reduce-scatter.14.cloned.1.call-update) | async-done | bytes 524304 | tf_op jit(solution)/shard_map/reduce_scatter | solution.py:284
  567.2 12.4 %fusion.84 = bf16[1,512,1024]{2,1,0:T(8,128)(2,1)} fusion(f32[1,512,1024]{2,1,0:T(8,128)S(1)} %get-tuple-element.270, bf16[4096,1024]{1,0:T(8,128)(2,1)} %all-gather.13.cloned.1.call-done, f32[1024]{0:T(1024)S(1)} %convert_element_type.245, f32[512,4096]{1,0:T(8,128)} %fusion.118, f32[4096]{0:T(1024)S(1)} %bitcast.304), kind=kOutput, calls=%fused_computation.120 | convolution fusion | flops 4317511680 | bytes 19943424 | tf_op jit(solution)/shard_map/dot_general | solution.py:160
  581.8 45.3 %reduce-scatter.6.cloned.1.call-done = bf16[16,1024]{1,0:T(8,128)(2,1)} async-done(((bf16[256,1024]{1,0:T(8,128)(2,1)}), bf16[16,1024]{1,0:T(8,128)(2,1)}) %reduce-scatter.6.cloned.1.call-update) | async-done | bytes 32784 | tf_op jit(solution)/shard_map/reduce_scatter | solution.py:257
  627.1 9.1 %all-reduce.13 = (bf16[16,1024]{1,0:T(8,128)(2,1)S(1)}, bf16[64]{0:T(256)(128)(2,1)S(1)}, bf16[64]{0:T(256)(128)(2,1)S(1)}, bf16[64]{0:T(256)(128)(2,1)S(1)}, bf...) all-reduce(bf16[16,1024]{1,0:T(8,128)(2,1)} %reduce-scatter.6.clone, ...), channel_id=1, replica_groups=mesh['dp'=2,'fsdp'=16] {'dp'}, use_global_device_ids=true, to_apply=%region_18.19 | all-reduce | flops 16960 | bytes 67840 | tf_op jit(solution)/shard_map/psum | solution.py:294
  639.9 75.2 %reduce-scatter.8.cloned.1.call-done = bf16[64,3072]{1,0:T(8,128)(2,1)} async-done(((bf16[1024,3072]{1,0:T(8,128)(2,1)}), bf16[64,3072]{1,0:T(8,128)(2,1)}) %reduce-scatter.8.cloned.1.call-update) | async-done | bytes 393232 | tf_op jit(solution)/shard_map/reduce_scatter | solution.py:266
  715.1 15.3 %all-gather = bf16[128,3072]{1,0:T(8,128)(2,1)S(1)} all-gather(bf16[64,3072]{1,0:T(8,128)(2,1)} %reduce-scatter.8.cloned.1.call-done), channel_id=2, replica_groups=mesh['dp'=2,'fsdp'=16] {'dp'}, dimensions={0}, use_global_device_ids=true | all-gather | bytes 1179648 | tf_op jit(solution)/shard_map/all_gather | solution.py:12
  731.7 29.7 %all-reduce.17.cloned.1.call-done = (bf16[64,1024]{1,0:T(8,128)(2,1)}, bf16[64,4096]{1,0:T(8,128)(2,1)}, bf16[256,1024]{1,0:T(8,128)(2,1)}) async-done(((bf16[64,1024]{1,0:T(8,128)(2,1)}, bf16[64,4096]{1,0:T(8,128)(2,1)}, bf16[256,1024]{1,0:T(8,128)(2,1)}), (bf16[64,1024]{1,0:T(8,128)(2,1)}, bf16[64,4096]{1,0:T(8,128)(2,1)}, bf16[256,1024]{1,0:T(8,128)(2,1)})) %all-reduce.17.cloned.1.call-update) | async-done | bytes 1179664 | tf_op jit(solution)/shard_map/psum | solution.py:298
  (240 shorter events, 152.1 us)
Async XLA Ops:
  7.2 65.0 %copy-start.2 = (bf16[1,512,1024]{2,1,0:T(8,128)(2,1)S(1)}, bf16[1,512,1024]{2,1,0:T(8,128)(2,1)}, u32[]{:S(2)}) copy-start(bf16[1,512,1024]{2,1,0:T(8,128)(2,1)} %param.19) | copy-start | bytes 3145732
  7.2 65.7 %copy-start.12 = (bf16[16,1024]{1,0:T(8,128)(2,1)S(1)}, bf16[16,1024]{1,0:T(8,128)(2,1)}, u32[]{:S(2)}) copy-start(bf16[16,1024]{1,0:T(8,128)(2,1)} %param.23) | copy-start | bytes 98308
  7.2 87.7 %all-gather.7.cloned.1.call-start = ((), (), s32[]{:S(2)}) async-start(), calls=%async_computation.5 | async-start | bytes 6684672 | tf_op jit(solution)/shard_map/all_gather | solution.py:99
  7.9 138.5 %all-gather.9.cloned.1.call-start = ((), (), s32[]{:S(2)}) async-start(), calls=%async_computation.6 | async-start | bytes 2228224 | tf_op jit(solution)/shard_map/all_gather | solution.py:100
  8.7 86.0 %copy-start.13 = (bf16[1,256]{1,0:T(2,128)(2,1)S(1)}, bf16[1,256]{1,0:T(2,128)(2,1)}, u32[]{:S(2)}) copy-start(bf16[1,256]{1,0:T(2,128)(2,1)} %param.21) | copy-start | bytes 1540
  8.7 184.2 %all-gather.11.cloned.1.call-start = ((), (), s32[]{:S(2)}) async-start(), calls=%async_computation.7 | async-start | bytes 8912896 | tf_op jit(solution)/shard_map/all_gather | solution.py:105
  9.4 258.4 %all-gather.13.cloned.1.call-start = ((), (), s32[]{:S(2)}) async-start(), calls=%async_computation.8 | async-start | bytes 8912896 | tf_op jit(solution)/shard_map/all_gather | solution.py:107
  10.0 488.3 %reduce-scatter.10.cloned.1.call-start = ((), (), s32[]{:S(2)}) async-start(), calls=%async_computation.11 | async-start | bytes 2228224 | tf_op jit(solution)/shard_map/reduce_scatter | solution.py:269
  146.3 1.0 copy-start.6
  146.4 1.3 copy-start.7
  267.9 13.7 %copy-start.14 = (bf16[1024,4096]{1,0:T(8,128)(2,1)S(1)}, bf16[1024,4096]{1,0:T(8,128)(2,1)}, u32[]{:S(2)}) copy-start(bf16[1024,4096]{1,0:T(8,128)(2,1)} %all-gather.11.cloned.1.call-done) | copy-start | bytes 25165828
  281.5 5.2 copy-start.16
  286.7 1.2 copy-start.8
  288.0 2.3 copy-start.9
  288.9 1.3 copy-start.4
  292.9 205.4 %reduce-scatter.12.cloned.1.call-start = ((), (), s32[]{:S(2)}) async-start(), calls=%async_computation.12 | async-start | bytes 8912896 | tf_op jit(solution)/shard_map/reduce_scatter | solution.py:278
  302.3 264.8 %reduce-scatter.14.cloned.1.call-start = ((), (), s32[]{:S(2)}) async-start(), calls=%async_computation.13 | async-start | bytes 8912896 | tf_op jit(solution)/shard_map/reduce_scatter | solution.py:284
  322.9 304.2 %reduce-scatter.6.cloned.1.call-start = ((), (), s32[]{:S(2)}) async-start(), calls=%async_computation.9 | async-start | bytes 557056 | tf_op jit(solution)/shard_map/reduce_scatter | solution.py:257
  409.7 1.6 copy-start
  409.7 2.2 copy-start.1
  413.1 1.3 copy-start.10
  413.1 3.2 slice-start
  414.4 3.5 slice-start.1
  424.4 290.8 %reduce-scatter.8.cloned.1.call-start = ((), (), s32[]{:S(2)}) async-start(), calls=%async_computation.10 | async-start | bytes 6684672 | tf_op jit(solution)/shard_map/reduce_scatter | solution.py:266
  432.6 1.4 copy-start.15
  432.6 328.8 %all-reduce.17.cloned.1.call-start = ((), (), s32[]{:S(2)}) async-start(), calls=%async_computation.14 | async-start | bytes 2359296 | tf_op jit(solution)/shard_map/psum | solution.py:298
  567.2 12.8 %copy-start.3 = (f32[512,1024]{1,0:T(8,128)S(1)}, f32[512,1024]{1,0:T(8,128)}, u32[]{:S(2)}) copy-start(f32[512,1024]{1,0:T(8,128)} %get-tuple-element.272) | copy-start | bytes 6291460
  567.2 12.8 %copy-start.5 = (f32[1,512,1024]{2,1,0:T(8,128)S(1)}, f32[1,512,1024]{2,1,0:T(8,128)}, u32[]{:S(2)}) copy-start(f32[1,512,1024]{2,1,0:T(8,128)} %copy-done.4) | copy-start | bytes 6291460
  761.4 3.8 copy-start.11
Sparse Core Ops, SparseCore 0:
  10.3 64.5 all-gather.6
  77.0 40.6 all-gather.8
  119.9 73.0 all-gather.10
  195.0 72.8 all-gather.12
  293.0 60.3 reduce-scatter.9
  357.3 102.5 reduce-scatter.11
  464.0 103.0 reduce-scatter.13
  571.3 55.8 reduce-scatter.5
  631.0 84.0 reduce-scatter.7
  717.4 43.9 all-reduce.16
